TPU v7x, 32 devices: a whole 2x2x4 slice. The times are simulated.
32 devices in a mesh: rep: 8 (over y, x, core), zero: 4 (over z).
Axes of the slice: x: 2, y: 2, z: 4, core: 2. Of those that a mesh axis runs over, the one named last changes fastest.
Arguments:
- grads: bfloat16 [8, 4, 4194304], P('rep', 'zero'), may hold values from -6 to 6
- master: float32 [8, 4194304], P('rep', 'zero'), may hold values from -6 to 6
- moment_one: float32 [8, 4194304], P('rep', 'zero'), may hold values from -0.4375 to 0.4375
- moment_two: float32 [8, 4194304], P('rep', 'zero'), may hold values from 0.0001 to 0.01
- step_index: int32 [1], replicated, may hold values from 0 to 999
Outputs:
- master_out: float32 [8, 4194304], P('rep', 'zero')
- moment_one_out: float32 [8, 4194304], P('rep', 'zero')
- moment_two_out: float32 [8, 4194304], P('rep', 'zero')
- params_out: bfloat16 [8, 4194304], P('rep')
All inputs are finite; a program needn't handle non-finite values.
Results may differ from a plain program's by a relative error of at most 0.0075.
Values may be sent and summed in bfloat16 or wider, within the bound.
No kernel may reach another device: no remote copies, remote signals or barrier semaphores. Data moves between devices by JAX's collectives and lax.ppermute only.
A program may use at most 192 MiB of HBM per device.

v0:
```python
import jax
import jax.numpy as jnp
from jax import lax
from jax.sharding import PartitionSpec as P


def swapped(value, axis, apart):
    mask = 2**apart
    pairs = [(source, source ^ mask) for source in range(lax.axis_size(axis))]
    return lax.ppermute(value, axis, pairs)


def partner_values(values, tstep):
    nbits = lax.axis_size("rep").bit_length() - 1
    bit = tstep % nbits
    result = jnp.zeros_like(values)
    for level in range(nbits):
        other = swapped(values, "rep", level)
        result = jnp.where(bit == level, other, result)
    return result


def shards(grads, master, moment_one, moment_two, step_index):
    loop_size = lax.axis_size("zero")
    terms = grads[0, 0].astype(jnp.float32)
    g = (
        lax.psum_scatter(
            terms.astype(jnp.bfloat16), "zero", scatter_dimension=0, tiled=True
        ).astype(jnp.float32)
        / loop_size
    )
    g = g[None, :]
    tstep = step_index[0]
    count = (tstep + 1).astype(jnp.float32)
    m_new = 0.9 * moment_one + 0.1 * g
    v_new = 0.999 * moment_two + 0.001 * g * g
    corr_one = 1.0 - jnp.power(jnp.float32(0.9), count)
    corr_two = 1.0 - jnp.power(jnp.float32(0.999), count)
    fresh = master - 0.02 * (m_new / corr_one / (jnp.sqrt(v_new / corr_two) + 1e-08) + 0.1 * master)
    averaged = 0.5 * (fresh + partner_values(fresh, tstep))
    whole = lax.all_gather(averaged.astype(jnp.bfloat16), "zero", axis=1, tiled=True)
    return (averaged, m_new, v_new, whole)


def solution(mesh):
    return jax.shard_map(
        shards,
        mesh=mesh,
        in_specs=(
            P("rep", "zero", None),
            P("rep", "zero"),
            P("rep", "zero"),
            P("rep", "zero"),
            P(),
        ),
        out_specs=(P("rep", "zero"), P("rep", "zero"), P("rep", "zero"), P("rep", None)),
        check_vma=False,
    )
```

profile of v0, /device:TPU:0, one launch (start us, length us, event | category | flops | bytes accessed | tf_op | source)
XLA Modules:
  0.0 927.4 jit_solution(12522624360998154430)
XLA Ops:
  7.2 0.0 all-reduce.3.cloned.1.call-start
  7.2 178.5 %reduce = bf16[4194304]{0:T(1024)(128)(2,1)} reduce(bf16[1,1,4194304]{2,1,0:T(2,128)(2,1)} %param.5, bf16[]{:T(256)} %constant.59), dimensions={0,1}, to_apply=%param.5.reduce_sub_computation | reduce | bytes 16777218 | tf_op args[0]
  185.7 0.0 copy-start.2
  185.7 0.0 all-reduce.3.cloned.1.call-update
  185.7 0.2 all-gather.2.cloned.1.call-start
  186.7 0.0 copy-done.2
  186.7 0.6 dynamic-slice
  187.9 291.5 %all-reduce.3.cloned.1.call-done = bf16[4194304]{0:T(1024)(128)(2,1)} async-done(((bf16[4194304]{0:T(1024)(128)(2,1)}), bf16[4194304]{0:T(1024)(128)(2,1)}) %all-reduce.3.cloned.1.call-update) | async-done | bytes 8388624
  479.4 0.0 copy-start
  479.4 0.0 copy-start.1
  479.4 2.4 convert_multiply_fusion.2
  481.9 0.4 copy-done
  482.3 1.3 copy-done.1
  483.5 24.8 %multiply_subtract_fusion = (f32[1,1048576]{1,0:T(1,128)}, f32[1,1048576]{1,0:T(1,128)}, f32[1,1048576]{1,0:T(1,128)}) fusion(f32[1,1048576]{1,0:T(1,128)S(1)} %copy-done, f32[]{:T(128)} %bitcast.4, f32[]{:T(128)} %bitcast.2, f32[1,1048576]{1,0:T(1,128)S(1)} %bitcast.7, f32[1,1048576]{1,0:T(1,128)S(1)} %copy-done.1, f32[1,1048576]{1,0:T(1,128)S(1)} %bitcast.6, ...), kind=kLoop, calls=%fused_computation.9 | loop fusion | flops 12582912 | bytes 33554440 | tf_op jit(solution)/shard_map/sub | solution.py:39
  508.3 0.0 collective-permute-start.2
  508.3 1.5 collective-permute-start.1
  509.8 1.5 collective-permute-start
  511.3 4.6 collective-permute-done.2
  515.8 85.8 %collective-permute-done.1 = f32[1,1048576]{1,0:T(1,128)} collective-permute-done((f32[1,1048576]{1,0:T(1,128)}, f32[1,1048576]{1,0:T(1,128)}, u32[]{:S(2)}, u32[]{:S(2)}) %collective-permute-start.1) | collective-permute-done | bytes 4194336 | tf_op jit(solution)/shard_map/ppermute | solution.py:10
  601.6 1.2 collective-permute-done
  602.8 12.9 %fusion.3 = (bf16[1,1048576]{1,0:T(2,128)(2,1)}, f32[1,1048576]{1,0:T(1,128)}) fusion(f32[1,1048576]{1,0:T(1,128)} %get-tuple-element.6, f32[1,1048576]{1,0:T(1,128)} %collective-permute-done, f32[1,1048576]{1,0:T(1,128)} %collective-permute-done.1, f32[1,1048576]{1,0:T(1,128)} %collective-permute-done.2, pred[]{:T(512)S(6)} %eq.13, pred[]{:T(512)S(6)} %eq.12, ...), kind=kLoop, calls=%fused_computation.12 | loop fusion | flops 6291456 | bytes 23068676 | tf_op jit(solution)/shard_map/convert_element_type | solution.py:41
  615.7 0.0 all-gather.2.cloned.1.call-update
  615.7 285.0 %all-gather.2.cloned.1.call-done = bf16[1,4194304]{1,0:T(2,128)(2,1)} async-done(((bf16[1,1048576]{1,0:T(2,128)(2,1)}), bf16[1,4194304]{1,0:T(2,128)(2,1)}) %all-gather.2.cloned.1.call-update) | async-done | bytes 8388624 | tf_op jit(solution)/shard_map/all_gather | solution.py:41
  900.7 19.8 %copy.12 = bf16[1,4194304]{1,0:T(2,128)(2,1)} copy(bf16[1,4194304]{1,0:T(2,128)(2,1)} %all-gather.2.cloned.1.call-done) | data formatting | bytes 16777216
Async XLA Ops:
  7.2 472.3 %all-reduce.3.cloned.1.call-start = ((), (), s32[]{:S(2)}) async-start(), calls=%async_computation.1 | async-start | bytes 16777216
  185.7 1.0 copy-start.2
  185.7 715.0 %all-gather.2.cloned.1.call-start = ((), (), s32[]{:S(2)}) async-start(), calls=%async_computation | async-start | bytes 20971520 | tf_op jit(solution)/shard_map/all_gather | solution.py:41
  479.4 2.8 copy-start
  479.4 4.1 copy-start.1
  508.3 7.5 collective-permute-start.2
  508.3 93.3 %collective-permute-start.1 = (f32[1,1048576]{1,0:T(1,128)}, f32[1,1048576]{1,0:T(1,128)}, u32[]{:S(2)}, u32[]{:S(2)}) collective-permute-start(f32[1,1048576]{1,0:T(1,128)} %get-tuple-element.6), channel_id=1, source_target_pairs={{0,8},{4,12},{8,0},{12,4},{16,24},{20,28},{24,16},{28,20},{1,9},{5... | collective-permute-start | bytes 12582920 | tf_op jit(solution)/shard_map/ppermute | solution.py:10
  509.8 93.0 %collective-permute-start = (f32[1,1048576]{1,0:T(1,128)}, f32[1,1048576]{1,0:T(1,128)}, u32[]{:S(2)}, u32[]{:S(2)}) collective-permute-start(f32[1,1048576]{1,0:T(1,128)} %get-tuple-element.6), channel_id=1, source_target_pairs={{0,16},{4,20},{8,24},{12,28},{16,0},{20,4},{24,8},{28,12},{1,17},{... | collective-permute-start | bytes 12582920 | tf_op jit(solution)/shard_map/ppermute | solution.py:10
Sparse Core Ops, SparseCore 0:
  185.8 293.5 all-reduce.2
  615.8 284.8 all-gather.1
where the time goes:
time: 928 us; the launch traced here: 927 us
  waiting for transfers between devices  668 us (72%)
  other arithmetic  219 us (24%)
  local copies, waits for them, and re-layouts  22.1 us (2%)
  between operations  15.4 us (2%)
    unnamed x3, waiting for transfers between devices  292 us
    all_gather x1, waiting for transfers between devices, shards(): lax.all_gather(averaged.astype(jnp.bfloat16), 'zero', axis=1, tiled=True)  285 us
    unnamed x1, other arithmetic  178 us
    ppermute x3, waiting for transfers between devices, swapped(): return lax.ppermute(value, axis, pairs)  91.5 us
    sub x1, other arithmetic, shards(): master - 0.02 * (m_new / corr_one / (jnp.sqrt(v_new / corr_two) + 1e-08)...  24.8 us
    unnamed x8, local copies, waits for them, and re-layouts  22.1 us
  transfers between devices with their start and end apart: 5, of which 5 were waited for; matrix products, arithmetic and copies ran while one was open for 0% of the time, Pallas kernels for 0%

commit v1 on v0

--- a/solution.py
+++ b/solution.py
@@ -2,6 +2,25 @@
 import jax.numpy as jnp
 from jax import lax
 from jax.sharding import PartitionSpec as P
+
+
+def joined_along(tiles, dim):
+    lengths = list(tiles.shape[1:])
+    lengths[dim] *= tiles.shape[0]
+    return jnp.moveaxis(tiles, 0, dim).reshape(lengths)
+
+
+def collected_by_bits(x, axis):
+    length, mine = (lax.axis_size(axis), lax.axis_index(axis))
+    tiles, bit = (x[None], 1)
+    while bit < length:
+        partner_block = lax.ppermute(tiles, axis, [(i, i ^ bit) for i in range(length)])
+        low = mine & bit == 0
+        tiles = jnp.concatenate(
+            [jnp.where(low, tiles, partner_block), jnp.where(low, partner_block, tiles)]
+        )
+        bit *= 2
+    return tiles
 
 
 def swapped(value, axis, apart):
@@ -38,7 +57,8 @@
     corr_two = 1.0 - jnp.power(jnp.float32(0.999), count)
     fresh = master - 0.02 * (m_new / corr_one / (jnp.sqrt(v_new / corr_two) + 1e-08) + 0.1 * master)
     averaged = 0.5 * (fresh + partner_values(fresh, tstep))
-    whole = lax.all_gather(averaged.astype(jnp.bfloat16), "zero", axis=1, tiled=True)
+    x = averaged.astype(jnp.bfloat16)
+    whole = joined_along(collected_by_bits(x, "zero"), 1)
     return (averaged, m_new, v_new, whole)
 
 

time: 928 us -> 993 us (1.070)
  other arithmetic: 219 us -> 261 us
  local copies, waits for them, and re-layouts: 22.1 us -> 55.8 us
  waiting for transfers between devices: 668 us -> 656 us
    all_gather x1 -> x0, waiting for transfers between devices: 285 us -> none  [shards(): lax.all_gather(averaged.astype(jnp.bfloat16), 'zero', axis=1, tiled=True)]
    ppermute x0 -> x2, waiting for transfers between devices: none -> 273 us  [collected_by_bits(): lax.ppermute(tiles, axis, [(i, i ^ bit) for i in range(length)])]
    unnamed x8 -> x12, local copies, waits for them, and re-layouts: 22.1 us -> 55.8 us
    select_n x0 -> x2, other arithmetic: none -> 23.4 us  [collected_by_bits(): jnp.where(low, tiles, partner_block)]
    broadcast_in_dim x0 -> x1, other arithmetic: none -> 12.9 us  [collected_by_bits(): tiles, bit = (x[None], 1)]
    convert_element_type x1 -> x0, other arithmetic: 12.9 us -> none  [shards(): averaged.astype(jnp.bfloat16)]
    concatenate x0 -> x1, other arithmetic: none -> 10.7 us  [collected_by_bits(): jnp.concatenate([jnp.where(low, tiles, partner_block), jnp.where(low, par...]
    unnamed x1 -> x2, other arithmetic: 178 us -> 187 us
  transfers between devices with their start and end apart: 5 -> 6, of which waited for: 5 -> 6; matrix products, arithmetic and copies ran while one was open for 0% -> 0% of each run, Pallas kernels for 0% -> 0%
where the time goes in v1:
time: 993 us
  waiting for transfers between devices  656 us (66%)
  other arithmetic  261 us (26%)
  local copies, waits for them, and re-layouts  55.8 us (6%)
  between operations  15.5 us (2%)
    unnamed x2, waiting for transfers between devices  292 us
    ppermute x2, waiting for transfers between devices, collected_by_bits(): lax.ppermute(tiles, axis, [(i, i ^ bit) for i in range(length)])  273 us
    unnamed x2, other arithmetic  187 us
    ppermute x3, waiting for transfers between devices, swapped(): return lax.ppermute(value, axis, pairs)  91.5 us
    unnamed x12, local copies, waits for them, and re-layouts  55.8 us
    sub x1, other arithmetic, shards(): master - 0.02 * (m_new / corr_one / (jnp.sqrt(v_new / corr_two) + 1e-08)...  24.8 us
    select_n x2, other arithmetic, collected_by_bits(): jnp.where(low, tiles, partner_block)  23.4 us
  transfers between devices with their start and end apart: 6, of which 6 were waited for; matrix products, arithmetic and copies ran while one was open for 0% of the time, Pallas kernels for 0%

profile of v1, /device:TPU:0, one launch (start us, length us, event | category | flops | bytes accessed | tf_op | source)
XLA Modules:
  0.0 993.3 jit_solution(11359143375554369221)
XLA Ops:
  7.2 0.0 all-reduce.3.cloned.1.call-start
  7.2 178.5 %reduce = bf16[4194304]{0:T(1024)(128)(2,1)} reduce(bf16[1,1,4194304]{2,1,0:T(2,128)(2,1)} %param.5, bf16[]{:T(256)} %constant.63), dimensions={0,1}, to_apply=%param.5.reduce_sub_computation | reduce | bytes 16777218 | tf_op args[0]
  185.7 0.0 copy-start.4
  185.7 0.0 all-reduce.3.cloned.1.call-update
  186.5 0.0 copy-done.4
  186.5 0.6 dynamic-slice
  187.7 291.7 %all-reduce.3.cloned.1.call-done = bf16[4194304]{0:T(1024)(128)(2,1)} async-done(((bf16[4194304]{0:T(1024)(128)(2,1)}), bf16[4194304]{0:T(1024)(128)(2,1)}) %all-reduce.3.cloned.1.call-update) | async-done | bytes 8388624
  479.4 0.0 copy-start.2
  479.4 0.0 copy-start.3
  479.4 2.4 convert_multiply_fusion.2
  481.9 0.4 copy-done.2
  482.3 1.3 copy-done.3
  483.5 24.8 %multiply_subtract_fusion = (f32[1,1048576]{1,0:T(1,128)}, f32[1,1048576]{1,0:T(1,128)}, f32[1,1048576]{1,0:T(1,128)}) fusion(f32[1,1048576]{1,0:T(1,128)S(1)} %copy-done.2, f32[]{:T(128)} %bitcast.4, f32[]{:T(128)} %bitcast.2, f32[1,1048576]{1,0:T(1,128)S(1)} %bitcast.17, f32[1,1048576]{1,0:T(1,128)S(1)} %copy-done.3, f32[1,1048576]{1,0:T(1,128)S(1)} %bitcast.16, ...), kind=kLoop, calls=%fused_computation.16 | loop fusion | flops 12582912 | bytes 33554440 | tf_op jit(solution)/shard_map/sub | solution.py:58
  508.3 0.0 collective-permute-start.2
  508.3 1.5 collective-permute-start.1
  509.8 1.5 collective-permute-start
  511.3 4.6 collective-permute-done.2
  515.8 85.8 %collective-permute-done.1 = f32[1,1048576]{1,0:T(1,128)} collective-permute-done((f32[1,1048576]{1,0:T(1,128)}, f32[1,1048576]{1,0:T(1,128)}, u32[]{:S(2)}, u32[]{:S(2)}) %collective-permute-start.1) | collective-permute-done | bytes 4194336 | tf_op jit(solution)/shard_map/ppermute | solution.py:29
  601.6 1.2 collective-permute-done
  602.8 12.9 %convert_bitcast_fusion = (bf16[1,1,1048576]{2,0,1:T(2,128)(2,1)}, f32[1,1048576]{1,0:T(1,128)}) fusion(f32[1,1048576]{1,0:T(1,128)} %get-tuple-element.6, f32[1,1048576]{1,0:T(1,128)} %collective-permute-done, f32[1,1048576]{1,0:T(1,128)} %collective-permute-done.1, f32[1,1048576]{1,0:T(1,128)} %collective-permute-done.2, pred[]{:T(512)S(6)} %eq.19, ...), kind=kLoop, calls=%fused_computation.15 | loop fusion | flops 6291456 | bytes 23068676 | tf_op jit(solution)/shard_map/broadcast_in_dim | solution.py:15
  615.7 0.0 collective-permute-start.3
  615.7 92.1 %collective-permute-done.3 = bf16[1,1,1048576]{2,0,1:T(2,128)(2,1)} collective-permute-done((bf16[1,1,1048576]{2,0,1:T(2,128)(2,1)}, bf16[1,1,1048576]{2,0,1:T(2,128)(2,1)}, u32[]{:S(2)}, u32[]{:S(2)}) %collective-permute-start.3) | collective-permute-done | bytes 2097184 | tf_op jit(solution)/shard_map/ppermute | solution.py:17
  707.9 8.9 broadcast_select_fusion.1
  716.8 0.0 copy-start
  716.8 0.0 copy-start.1
  716.8 10.7 %pad_maximum_fusion = bf16[2,1,1048576]{2,0,1:T(2,128)(2,1)} fusion(bf16[1,1,1048576]{2,0,1:T(2,128)(2,1)S(1)} %get-tuple-element.12, bf16[1,1,1048576]{2,0,1:T(2,128)(2,1)S(1)} %get-tuple-element.11), kind=kLoop, calls=%fused_computation.14 | loop fusion | flops 8388608 | bytes 8388608 | tf_op jit(solution)/shard_map/concatenate | solution.py:19
  727.5 0.0 copy-done
  727.5 0.0 copy-done.1
  727.5 1.4 collective-permute-start.4
  728.9 180.7 %collective-permute-done.4 = bf16[2,1,1048576]{2,0,1:T(2,128)(2,1)} collective-permute-done((bf16[2,1,1048576]{2,0,1:T(2,128)(2,1)}, bf16[2,1,1048576]{2,0,1:T(2,128)(2,1)}, u32[]{:S(2)}, u32[]{:S(2)}) %collective-permute-start.4) | collective-permute-done | bytes 4194336 | tf_op jit(solution)/shard_map/ppermute | solution.py:17
  909.6 14.5 %broadcast_select_fusion.3 = (bf16[2,1,1048576]{2,0,1:T(2,128)(2,1)S(1)}, bf16[2,1,1048576]{2,0,1:T(2,128)(2,1)S(1)}) fusion(bf16[2,1,1048576]{2,0,1:T(2,128)(2,1)} %collective-permute-done.4, pred[]{:T(512)S(6)} %eq.20, bf16[1,1,1048576]{2,0,1:T(2,128)(2,1)} %copy-done.1, bf16[1,1,1048576]{2,0,1:T(2,128)(2,1)} %copy-done), kind=kLoop, calls=%fused_computation.4 | loop fusion | flops 12582912 | bytes 16777216 | tf_op jit(solution)/shard_map/jit(_where)/select_n | solution.py:20
  924.1 8.8 maximum_bitcast_fusion
  932.9 53.5 %copy.9 = bf16[1,1,4,1048576]{3,1,2,0:T(2,128)(2,1)} copy(bf16[1,1,4,1048576]{3,2,1,0:T(4,128)(2,1)S(1)} %maximum_bitcast_fusion) | data formatting | bytes 16777216
Async XLA Ops:
  7.2 472.3 %all-reduce.3.cloned.1.call-start = ((), (), s32[]{:S(2)}) async-start(), calls=%async_computation | async-start | bytes 16777216
  185.7 0.8 copy-start.4
  479.4 2.8 copy-start.2
  479.4 4.1 copy-start.3
  508.3 7.5 collective-permute-start.2
  508.3 93.3 %collective-permute-start.1 = (f32[1,1048576]{1,0:T(1,128)}, f32[1,1048576]{1,0:T(1,128)}, u32[]{:S(2)}, u32[]{:S(2)}) collective-permute-start(f32[1,1048576]{1,0:T(1,128)} %get-tuple-element.6), channel_id=1, source_target_pairs={{0,8},{4,12},{8,0},{12,4},{16,24},{20,28},{24,16},{28,20},{1,9},{5... | collective-permute-start | bytes 12582920 | tf_op jit(solution)/shard_map/ppermute | solution.py:29
  509.8 93.0 %collective-permute-start = (f32[1,1048576]{1,0:T(1,128)}, f32[1,1048576]{1,0:T(1,128)}, u32[]{:S(2)}, u32[]{:S(2)}) collective-permute-start(f32[1,1048576]{1,0:T(1,128)} %get-tuple-element.6), channel_id=1, source_target_pairs={{0,16},{4,20},{8,24},{12,28},{16,0},{20,4},{24,8},{28,12},{1,17},{... | collective-permute-start | bytes 12582920 | tf_op jit(solution)/shard_map/ppermute | solution.py:29
  615.7 92.2 %collective-permute-start.3 = (bf16[1,1,1048576]{2,0,1:T(2,128)(2,1)}, bf16[1,1,1048576]{2,0,1:T(2,128)(2,1)}, u32[]{:S(2)}, u32[]{:S(2)}) collective-permute-start(bf16[1,1,1048576]{2,0,1:T(2,128)(2,1)} %get-tuple-element.4), channel_id=1, source_target_pairs={{0,1},{1,0},{2,3},{3,2},{4,5},{5,4},{6,7},{7,6},{8,9},{9,8},{10,11... | collective-permute-start | bytes 6291464 | tf_op jit(solution)/shard_map/ppermute | solution.py:17
  716.8 10.7 %copy-start = (bf16[1,1,1048576]{2,0,1:T(2,128)(2,1)}, bf16[1,1,1048576]{2,0,1:T(2,128)(2,1)S(1)}, u32[]{:S(2)}) copy-start(bf16[1,1,1048576]{2,0,1:T(2,128)(2,1)S(1)} %get-tuple-element.11) | copy-start | bytes 6291460
  716.8 10.7 %copy-start.1 = (bf16[1,1,1048576]{2,0,1:T(2,128)(2,1)}, bf16[1,1,1048576]{2,0,1:T(2,128)(2,1)S(1)}, u32[]{:S(2)}) copy-start(bf16[1,1,1048576]{2,0,1:T(2,128)(2,1)S(1)} %get-tuple-element.12) | copy-start | bytes 6291460
  727.5 182.1 %collective-permute-start.4 = (bf16[2,1,1048576]{2,0,1:T(2,128)(2,1)}, bf16[2,1,1048576]{2,0,1:T(2,128)(2,1)}, u32[]{:S(2)}, u32[]{:S(2)}) collective-permute-start(bf16[2,1,1048576]{2,0,1:T(2,128)(2,1)} %pad_maximum_fusion), channel_id=1, source_target_pairs={{0,2},{1,3},{2,0},{3,1},{4,6},{5,7},{6,4},{7,5},{8,10},{9,11},{10,... | collective-permute-start | bytes 12582920 | tf_op jit(solution)/shard_map/ppermute | solution.py:17
Sparse Core Ops, SparseCore 0:
  185.8 293.5 all-reduce.2
